TPU v7x, 256 devices: a whole 4x4x8 slice. The times are simulated.
256 devices in a mesh: prow: 8 (over z), pcol: 32 (over x, y, core).
Axes of the slice: x: 4, y: 4, z: 8, core: 2. Of those that a mesh axis runs over, the one named last changes fastest.
Arguments:
- matrix: bfloat16 [8, 2048, 2, 8192], P(None, 'prow', None, 'pcol'), may hold values from -6 to 6
- pivots: int32 [4, 256], replicated, may hold values from 0 to 16383, as said below
- lower_inverse: bfloat16 [4, 256, 256], replicated, as said below
- upper_inverse: bfloat16 [4, 256, 256], replicated, as said below
Outputs:
- factored: bfloat16 [8, 2048, 2, 8192], P(None, 'prow', None, 'pcol')
Inputs may be any that keep to these rules, and one draw needn't show every extreme that they name: For step s and each i, pivots[s, i] is either s * 256 + i or a row index of s * 256 + 256 or more; the pivots of one step that differ from s * 256 + i are distinct. lower_inverse[s] is unit lower triangular. upper_inverse[s] is upper triangular.
All inputs are finite; a program needn't handle non-finite values.
Results may differ from a plain program's by a relative error of at most 0.0071.
Values may be sent and summed in bfloat16 or wider, within the bound.
A program may use at most 64 MiB of HBM per device.

v0:
```python
import jax
import jax.numpy as jnp
from jax import lax
from jax.sharding import PartitionSpec as P


def spread(value, axis, source):
    kept = jnp.where(lax.axis_index(axis) == source, value, 0).astype(value.dtype)
    return lax.psum(kept, axis)


def local(matrix, pivots, lower_inverse, upper_inverse):
    row_blocks = matrix.shape[0]
    block_size = matrix.shape[1]
    col_blocks = matrix.shape[2]
    local_rows = row_blocks * block_size
    local_cols = col_blocks * block_size
    matrix_loc = matrix.reshape(local_rows, local_cols)
    row_count = lax.axis_size("prow")
    col_count = lax.axis_size("pcol")
    my_row = lax.axis_index("prow")
    my_col = lax.axis_index("pcol")
    row_iota = jnp.arange(local_rows, dtype=jnp.int32)
    col_iota = jnp.arange(local_cols, dtype=jnp.int32)
    global_row = (row_iota // block_size * row_count + my_row) * block_size + row_iota % block_size
    global_col = (col_iota // block_size * col_count + my_col) * block_size + col_iota % block_size
    for step_num in range(pivots.shape[0]):
        begin_at = step_num * block_size
        trail_at = begin_at + block_size
        diag_root = step_num % row_count
        diag_local = step_num // row_count * block_size
        panel_root = step_num % col_count
        panel_local = step_num // col_count * block_size
        targets = begin_at + jnp.arange(block_size, dtype=jnp.int32)
        chosen = pivots[step_num]
        chosen_block = chosen // block_size
        chosen_owner = chosen_block % row_count
        is_mine = chosen_owner == my_row
        chosen_local = chosen_block // row_count * block_size + chosen % block_size
        picked = jnp.take(matrix_loc, jnp.where(is_mine, chosen_local, 0), axis=0)
        picked = jnp.where(is_mine[:, None], picked, jnp.zeros_like(picked))
        diag_rows = matrix_loc[diag_local : diag_local + block_size]
        gathered = lax.all_gather(picked, "prow", axis=0, tiled=True)
        stacked = gathered.reshape(row_count, block_size, local_cols)
        owner_hit = jnp.arange(row_count, dtype=jnp.int32)[:, None] == chosen_owner[None, :]
        new_rows = jnp.sum(
            jnp.where(owner_hit[:, :, None], stacked, jnp.zeros_like(stacked)), axis=0
        )
        old_diag = spread(diag_rows, "prow", diag_root)
        moved_rows = is_mine & (chosen != targets)
        matrix_loc = matrix_loc.at[jnp.where(moved_rows, chosen_local, local_rows)].set(
            old_diag, mode="drop"
        )
        diag_after = matrix_loc[diag_local : diag_local + block_size]
        matrix_loc = matrix_loc.at[diag_local : diag_local + block_size].set(
            jnp.where(my_row == diag_root, new_rows, diag_after)
        )
        upper_full = jnp.dot(
            lower_inverse[step_num], new_rows, preferred_element_type=jnp.float32
        ).astype(jnp.bfloat16)
        col_live = global_col >= trail_at
        upper_use = jnp.where(col_live[None, :], upper_full, jnp.zeros_like(upper_full))
        panel_own = matrix_loc[:, panel_local : panel_local + block_size]
        received = spread(panel_own, "pcol", panel_root)
        left_full = jnp.dot(
            received, upper_inverse[step_num], preferred_element_type=jnp.float32
        ).astype(jnp.bfloat16)
        row_live = global_row >= trail_at
        left_use = jnp.where(row_live[:, None], left_full, jnp.zeros_like(left_full))
        matrix_loc = (
            matrix_loc.astype(jnp.float32)
            - jnp.dot(left_use, upper_use, preferred_element_type=jnp.float32)
        ).astype(jnp.bfloat16)
        panel_now = matrix_loc[:, panel_local : panel_local + block_size]
        panel_put = jnp.where(row_live[:, None] & (my_col == panel_root), left_full, panel_now)
        matrix_loc = matrix_loc.at[:, panel_local : panel_local + block_size].set(panel_put)
        diag_now = matrix_loc[diag_local : diag_local + block_size]
        diag_put = jnp.where(col_live[None, :] & (my_row == diag_root), upper_full, diag_now)
        matrix_loc = matrix_loc.at[diag_local : diag_local + block_size].set(diag_put)
    return matrix_loc.reshape(matrix.shape)


def solution(mesh):
    placed = (P(None, "prow", None, "pcol"), P(), P(), P())
    return jax.shard_map(
        local, mesh=mesh, in_specs=placed, out_specs=P(None, "prow", None, "pcol"), check_vma=False
    )
```

profile of v0, /device:TPU:1, one launch (start us, length us, event | category | flops | bytes accessed | tf_op | source)
XLA Modules:
  0.0 982.3 jit_solution(12199594610326055330)
XLA Ops:
  6.5 1.2 broadcast_select_fusion
  8.5 0.9 and_select_fusion
  9.4 2.0 copy.17
  11.5 1.2 gather_fusion
  14.4 66.9 %all-reduce.9.cloned.1.call-done = bf16[256,512]{1,0:T(8,128)(2,1)} async-done(((bf16[256,512]{1,0:T(8,128)(2,1)}), bf16[256,512]{1,0:T(8,128)(2,1)}) %all-reduce.9.cloned.1.call-update) | async-done | bytes 262160 | tf_op jit(solution)/shard_map/psum | solution.py:9
  81.3 3.1 scatter_fusion
  84.4 38.9 %all-gather.5.cloned.1.call-done = bf16[2048,512]{1,0:T(8,128)(2,1)} async-done(((bf16[256,512]{1,0:T(8,128)(2,1)}), bf16[2048,512]{1,0:T(8,128)(2,1)}) %all-gather.5.cloned.1.call-update) | async-done | bytes 2097168 | tf_op jit(solution)/shard_map/all_gather | solution.py:43
  123.4 1.9 select_reduce_fusion.3
  125.3 1.0 slice_select_fusion.3
  126.7 118.0 %all-reduce.11.cloned.1.call-done = bf16[2048,256]{1,0:T(8,128)(2,1)} async-done(((bf16[2048,256]{1,0:T(8,128)(2,1)}), bf16[2048,256]{1,0:T(8,128)(2,1)}) %all-reduce.11.cloned.1.call-update) | async-done | bytes 1048592 | tf_op jit(solution)/shard_map/psum | solution.py:9
  244.7 1.6 convolution_convert_fusion.3
  246.4 2.0 subtract_convert_fusion.3
  248.4 3.4 fusion.4
  251.8 1.8 broadcast_select_fusion.3
  253.7 3.1 gather_fusion.1
  257.8 63.7 %all-reduce.13.cloned.1.call-done = bf16[256,512]{1,0:T(8,128)(2,1)} async-done(((bf16[256,512]{1,0:T(8,128)(2,1)}), bf16[256,512]{1,0:T(8,128)(2,1)}) %all-reduce.13.cloned.1.call-update) | async-done | bytes 262160 | tf_op jit(solution)/shard_map/psum | solution.py:9
  321.5 5.2 scatter_fusion.1
  326.7 36.7 %all-gather.7.cloned.1.call-done = bf16[2048,512]{1,0:T(8,128)(2,1)} async-done(((bf16[256,512]{1,0:T(8,128)(2,1)}), bf16[2048,512]{1,0:T(8,128)(2,1)}) %all-gather.7.cloned.1.call-update) | async-done | bytes 2097168 | tf_op jit(solution)/shard_map/all_gather | solution.py:43
  363.4 1.9 select_reduce_fusion.2
  365.2 1.7 fusion.23
  367.0 2.3 slice_select_fusion.2
  369.6 118.0 %all-reduce.15.cloned.1.call-done = bf16[2048,256]{1,0:T(8,128)(2,1)} async-done(((bf16[2048,256]{1,0:T(8,128)(2,1)}), bf16[2048,256]{1,0:T(8,128)(2,1)}) %all-reduce.15.cloned.1.call-update) | async-done | bytes 1048592 | tf_op jit(solution)/shard_map/psum | solution.py:9
  487.6 1.6 convolution_convert_fusion.2
  489.3 2.3 subtract_convert_fusion.2
  491.5 1.5 fusion.5
  494.1 1.2 gather_fusion.2
  496.2 65.4 %all-reduce.17.cloned.1.call-done = bf16[256,512]{1,0:T(8,128)(2,1)} async-done(((bf16[256,512]{1,0:T(8,128)(2,1)}), bf16[256,512]{1,0:T(8,128)(2,1)}) %all-reduce.17.cloned.1.call-update) | async-done | bytes 262160 | tf_op jit(solution)/shard_map/psum | solution.py:9
  561.6 3.1 scatter_fusion.2
  564.7 38.9 %all-gather.9.cloned.1.call-done = bf16[2048,512]{1,0:T(8,128)(2,1)} async-done(((bf16[256,512]{1,0:T(8,128)(2,1)}), bf16[2048,512]{1,0:T(8,128)(2,1)}) %all-gather.9.cloned.1.call-update) | async-done | bytes 2097168 | tf_op jit(solution)/shard_map/all_gather | solution.py:43
  603.6 1.9 select_reduce_fusion.1
  605.6 1.0 slice_select_fusion.1
  607.0 118.0 %all-reduce.19.cloned.1.call-done = bf16[2048,256]{1,0:T(8,128)(2,1)} async-done(((bf16[2048,256]{1,0:T(8,128)(2,1)}), bf16[2048,256]{1,0:T(8,128)(2,1)}) %all-reduce.19.cloned.1.call-update) | async-done | bytes 1048592 | tf_op jit(solution)/shard_map/psum | solution.py:9
  725.0 1.7 convolution_convert_fusion.1
  726.6 2.0 subtract_convert_fusion.1
  728.6 3.4 fusion.6
  732.0 1.8 broadcast_select_fusion.1
  734.0 3.1 gather_fusion.3
  738.0 63.7 %all-reduce.21.cloned.1.call-done = bf16[256,512]{1,0:T(8,128)(2,1)} async-done(((bf16[256,512]{1,0:T(8,128)(2,1)}), bf16[256,512]{1,0:T(8,128)(2,1)}) %all-reduce.21.cloned.1.call-update) | async-done | bytes 262160 | tf_op jit(solution)/shard_map/psum | solution.py:9
  801.7 5.2 scatter_fusion.3
  806.9 36.8 %all-gather.11.cloned.1.call-done = bf16[2048,512]{1,0:T(8,128)(2,1)} async-done(((bf16[256,512]{1,0:T(8,128)(2,1)}), bf16[2048,512]{1,0:T(8,128)(2,1)}) %all-gather.11.cloned.1.call-update) | async-done | bytes 2097168 | tf_op jit(solution)/shard_map/all_gather | solution.py:43
  843.8 1.9 select_reduce_fusion
  845.6 1.7 fusion.21
  847.4 2.3 slice_select_fusion
  850.0 118.0 %all-reduce.23.cloned.1.call-done = bf16[2048,256]{1,0:T(8,128)(2,1)} async-done(((bf16[2048,256]{1,0:T(8,128)(2,1)}), bf16[2048,256]{1,0:T(8,128)(2,1)}) %all-reduce.23.cloned.1.call-update) | async-done | bytes 1048592 | tf_op jit(solution)/shard_map/psum | solution.py:9
  968.0 1.6 convolution_convert_fusion
  969.7 2.3 subtract_convert_fusion
  971.9 1.5 fusion.7
  973.5 2.0 reshape.1320
  (69 shorter events, 8.0 us)
Async XLA Ops:
  6.5 74.8 %all-reduce.9.cloned.1.call-start = ((), (), s32[]{:S(2)}) async-start(), calls=%async_computation | async-start | bytes 524288 | tf_op jit(solution)/shard_map/psum | solution.py:9
  8.5 114.9 %all-gather.5.cloned.1.call-start = ((), (), s32[]{:S(2)}) async-start(), calls=%async_computation.1 | async-start | bytes 2359296 | tf_op jit(solution)/shard_map/all_gather | solution.py:43
  11.5 2.8 copy-start.1
  13.5 231.2 %all-reduce.11.cloned.1.call-start = ((), (), s32[]{:S(2)}) async-start(), calls=%async_computation.2 | async-start | bytes 2097152 | tf_op jit(solution)/shard_map/psum | solution.py:9
  125.2 1.3 copy-start
  126.4 195.1 %all-reduce.13.cloned.1.call-start = ((), (), s32[]{:S(2)}) async-start(), calls=%async_computation.3 | async-start | bytes 524288 | tf_op jit(solution)/shard_map/psum | solution.py:9
  253.6 109.7 %all-gather.7.cloned.1.call-start = ((), (), s32[]{:S(2)}) async-start(), calls=%async_computation.4 | async-start | bytes 2359296 | tf_op jit(solution)/shard_map/all_gather | solution.py:43
  257.6 230.0 %all-reduce.15.cloned.1.call-start = ((), (), s32[]{:S(2)}) async-start(), calls=%async_computation.5 | async-start | bytes 2097152 | tf_op jit(solution)/shard_map/psum | solution.py:9
  369.3 192.3 %all-reduce.17.cloned.1.call-start = ((), (), s32[]{:S(2)}) async-start(), calls=%async_computation.6 | async-start | bytes 524288 | tf_op jit(solution)/shard_map/psum | solution.py:9
  493.8 109.8 %all-gather.9.cloned.1.call-start = ((), (), s32[]{:S(2)}) async-start(), calls=%async_computation.7 | async-start | bytes 2359296 | tf_op jit(solution)/shard_map/all_gather | solution.py:43
  496.1 228.9 %all-reduce.19.cloned.1.call-start = ((), (), s32[]{:S(2)}) async-start(), calls=%async_computation.8 | async-start | bytes 2097152 | tf_op jit(solution)/shard_map/psum | solution.py:9
  606.7 195.1 %all-reduce.21.cloned.1.call-start = ((), (), s32[]{:S(2)}) async-start(), calls=%async_computation.9 | async-start | bytes 524288 | tf_op jit(solution)/shard_map/psum | solution.py:9
  733.9 109.9 %all-gather.11.cloned.1.call-start = ((), (), s32[]{:S(2)}) async-start(), calls=%async_computation.10 | async-start | bytes 2359296 | tf_op jit(solution)/shard_map/all_gather | solution.py:43
  737.9 230.1 %all-reduce.23.cloned.1.call-start = ((), (), s32[]{:S(2)}) async-start(), calls=%async_computation.11 | async-start | bytes 2097152 | tf_op jit(solution)/shard_map/psum | solution.py:9
Sparse Core Ops, SparseCore 0:
  9.6 71.6 all-reduce.8
  83.1 40.1 all-gather.4
  126.6 118.0 all-reduce.10
  253.8 67.6 all-reduce.12
  323.1 40.1 all-gather.6
  369.4 118.1 all-reduce.14
  494.0 67.5 all-reduce.16
  563.4 40.1 all-gather.8
  606.9 118.0 all-reduce.18
  734.0 67.6 all-reduce.20
  803.5 40.1 all-gather.10
  849.8 118.1 all-reduce.22
where the time goes:
time: 983 us; the launch traced here: 982 us
  waiting for transfers between devices  883 us (90%)
  other arithmetic  38.6 us (4%)
  local copies, waits for them, and re-layouts  29.8 us (3%)
  matrix products  16 us (2%)
  between operations  13.9 us (1%)
    psum x8, waiting for transfers between devices, spread(): return lax.psum(kept, axis)  732 us
    all_gather x4, waiting for transfers between devices, local(): gathered = lax.all_gather(picked, 'prow', axis=0, tiled=True)  151 us
  transfers between devices with their start and end apart: 12, of which 12 were waited for; matrix products, arithmetic and copies ran while one was open for 3% of the time, Pallas kernels for 0%

commit v1 on v0

--- a/solution.py
+++ b/solution.py
@@ -2,6 +2,13 @@
 import jax.numpy as jnp
 from jax import lax
 from jax.sharding import PartitionSpec as P
+
+
+def cut_the_terms(x_part, net_axis):
+    local_out = lax.axis_size(net_axis)
+    outer = jnp.stack([x_part] * local_out, 0)
+    prior = lax.all_to_all(outer, net_axis, 0, 0)
+    return jnp.concatenate(prior, 0)
 
 
 def spread(value, axis, source):
@@ -40,7 +47,7 @@
         picked = jnp.take(matrix_loc, jnp.where(is_mine, chosen_local, 0), axis=0)
         picked = jnp.where(is_mine[:, None], picked, jnp.zeros_like(picked))
         diag_rows = matrix_loc[diag_local : diag_local + block_size]
-        gathered = lax.all_gather(picked, "prow", axis=0, tiled=True)
+        gathered = cut_the_terms(picked, "prow")
         stacked = gathered.reshape(row_count, block_size, local_cols)
         owner_hit = jnp.arange(row_count, dtype=jnp.int32)[:, None] == chosen_owner[None, :]
         new_rows = jnp.sum(

time: 983 us -> 939 us (0.955)
  waiting for transfers between devices: 883 us -> 809 us
  starting transfers between devices: 0.64 us -> 29.7 us
    all_gather x4 -> x0, waiting for transfers between devices: 151 us -> none  [local(): gathered = lax.all_gather(picked, 'prow', axis=0, tiled=True)]
    psum x8, waiting for transfers between devices: 732 us -> 807 us  [spread(): return lax.psum(kept, axis)]
    all_to_all x0 -> x4, starting transfers between devices: none -> 29.3 us  [cut_the_terms(): prior = lax.all_to_all(outer, net_axis, 0, 0)]
  transfers between devices with their start and end apart: 12 -> 12, of which waited for: 12 -> 8; matrix products, arithmetic and copies ran while one was open for 3% -> 2% of each run, Pallas kernels for 0% -> 0%
where the time goes in v1:
time: 939 us; the launch traced here: 938 us
  waiting for transfers between devices  809 us (86%)
  local copies, waits for them, and re-layouts  35.9 us (4%)
  other arithmetic  33 us (4%)
  starting transfers between devices  29.7 us (3%)
  matrix products  16 us (2%)
  between operations  13.9 us (1%)
    psum x8, waiting for transfers between devices, spread(): return lax.psum(kept, axis)  807 us
    all_to_all x4, starting transfers between devices, cut_the_terms(): prior = lax.all_to_all(outer, net_axis, 0, 0)  29.3 us
  transfers between devices with their start and end apart: 12, of which 8 were waited for; matrix products, arithmetic and copies ran while one was open for 2% of the time, Pallas kernels for 0%

profile of v1, /device:TPU:1, one launch (start us, length us, event | category | flops | bytes accessed | tf_op | source)
XLA Modules:
  0.0 937.8 jit_solution(4130637239781943972)
XLA Ops:
  7.5 2.0 copy.21
  9.5 1.2 gather_fusion
  10.8 1.5 stack.8
  12.3 9.1 all-to-all-start
  21.5 1.2 broadcast_select_fusion
  24.3 82.9 %all-reduce.9.cloned.1.call-done = bf16[256,512]{1,0:T(8,128)(2,1)} async-done(((bf16[256,512]{1,0:T(8,128)(2,1)}), bf16[256,512]{1,0:T(8,128)(2,1)}) %all-reduce.9.cloned.1.call-update) | async-done | bytes 262160 | tf_op jit(solution)/shard_map/psum | solution.py:16
  107.2 3.1 scatter_fusion
  110.3 1.9 select_reduce_fusion.3
  112.3 1.0 slice_select_fusion.3
  113.6 118.8 %all-reduce.11.cloned.1.call-done = bf16[2048,256]{1,0:T(8,128)(2,1)} async-done(((bf16[2048,256]{1,0:T(8,128)(2,1)}), bf16[2048,256]{1,0:T(8,128)(2,1)}) %all-reduce.11.cloned.1.call-update) | async-done | bytes 1048592 | tf_op jit(solution)/shard_map/psum | solution.py:16
  232.4 1.7 convolution_convert_fusion.3
  234.1 2.0 subtract_convert_fusion.3
  236.1 3.4 fusion.4
  239.4 1.9 broadcast_select_fusion.3
  241.3 3.1 gather_fusion.1
  244.5 1.5 stack.9
  246.0 6.7 all-to-all-start.1
  253.6 83.1 %all-reduce.13.cloned.1.call-done = bf16[256,512]{1,0:T(8,128)(2,1)} async-done(((bf16[256,512]{1,0:T(8,128)(2,1)}), bf16[256,512]{1,0:T(8,128)(2,1)}) %all-reduce.13.cloned.1.call-update) | async-done | bytes 262160 | tf_op jit(solution)/shard_map/psum | solution.py:16
  336.7 5.2 scatter_fusion.1
  342.5 1.7 fusion.23
  344.2 2.3 slice_select_fusion.2
  346.8 118.7 %all-reduce.15.cloned.1.call-done = bf16[2048,256]{1,0:T(8,128)(2,1)} async-done(((bf16[2048,256]{1,0:T(8,128)(2,1)}), bf16[2048,256]{1,0:T(8,128)(2,1)}) %all-reduce.15.cloned.1.call-update) | async-done | bytes 1048592 | tf_op jit(solution)/shard_map/psum | solution.py:16
  465.5 1.6 convolution_convert_fusion.2
  467.2 2.3 subtract_convert_fusion.2
  469.5 1.4 fusion.5
  471.7 1.2 gather_fusion.2
  473.0 1.5 stack.10
  474.5 6.7 all-to-all-start.2
  481.9 83.3 %all-reduce.17.cloned.1.call-done = bf16[256,512]{1,0:T(8,128)(2,1)} async-done(((bf16[256,512]{1,0:T(8,128)(2,1)}), bf16[256,512]{1,0:T(8,128)(2,1)}) %all-reduce.17.cloned.1.call-update) | async-done | bytes 262160 | tf_op jit(solution)/shard_map/psum | solution.py:16
  565.2 3.1 scatter_fusion.2
  568.4 1.9 select_reduce_fusion.1
  571.7 118.7 %all-reduce.19.cloned.1.call-done = bf16[2048,256]{1,0:T(8,128)(2,1)} async-done(((bf16[2048,256]{1,0:T(8,128)(2,1)}), bf16[2048,256]{1,0:T(8,128)(2,1)}) %all-reduce.19.cloned.1.call-update) | async-done | bytes 1048592 | tf_op jit(solution)/shard_map/psum | solution.py:16
  690.4 1.7 convolution_convert_fusion.1
  692.0 2.0 subtract_convert_fusion.1
  694.0 3.4 fusion.6
  697.4 1.9 broadcast_select_fusion.1
  699.2 3.1 gather_fusion.3
  702.5 1.5 stack.11
  704.0 6.7 all-to-all-start.3
  711.6 83.1 %all-reduce.21.cloned.1.call-done = bf16[256,512]{1,0:T(8,128)(2,1)} async-done(((bf16[256,512]{1,0:T(8,128)(2,1)}), bf16[256,512]{1,0:T(8,128)(2,1)}) %all-reduce.21.cloned.1.call-update) | async-done | bytes 262160 | tf_op jit(solution)/shard_map/psum | solution.py:16
  794.6 5.2 scatter_fusion.3
  800.4 1.7 fusion.21
  802.2 2.3 slice_select_fusion
  804.8 118.7 %all-reduce.23.cloned.1.call-done = bf16[2048,256]{1,0:T(8,128)(2,1)} async-done(((bf16[2048,256]{1,0:T(8,128)(2,1)}), bf16[2048,256]{1,0:T(8,128)(2,1)}) %all-reduce.23.cloned.1.call-update) | async-done | bytes 1048592 | tf_op jit(solution)/shard_map/psum | solution.py:16
  923.5 1.7 convolution_convert_fusion
  925.2 2.2 subtract_convert_fusion
  927.4 1.4 fusion.7
  928.9 2.0 reshape.1312
  (68 shorter events, 9.6 us)
Async XLA Ops:
  12.3 11.9 %copy-start.1 = (s32[4,256]{1,0:T(4,128)S(1)}, s32[4,256]{1,0:T(4,128)}, u32[]{:S(2)}) copy-start(s32[4,256]{1,0:T(4,128)} %param.31) | copy-start | bytes 12292
  12.3 98.0 %all-to-all-start = ((bf16[8,256,512]{2,1,0:T(8,128)(2,1)}), bf16[8,256,512]{2,1,0:T(8,128)(2,1)}, u32[]{:S(2)}, u32[]{:S(2)}) async-start(bf16[8,256,512]{2,1,0:T(8,128)(2,1)} %stack.8), calls=%async_computation | async-start | bytes 4194304 | tf_op jit(solution)/shard_map/all_to_all | solution.py:10
  21.4 85.8 %all-reduce.9.cloned.1.call-start = ((), (), s32[]{:S(2)}) async-start(), calls=%async_computation.4 | async-start | bytes 524288 | tf_op jit(solution)/shard_map/psum | solution.py:16
  23.4 209.0 %all-reduce.11.cloned.1.call-start = ((), (), s32[]{:S(2)}) async-start(), calls=%async_computation.5 | async-start | bytes 2097152 | tf_op jit(solution)/shard_map/psum | solution.py:16
  112.2 1.2 copy-start
  246.0 95.8 %all-to-all-start.1 = ((bf16[8,256,512]{2,1,0:T(8,128)(2,1)}), bf16[8,256,512]{2,1,0:T(8,128)(2,1)S(1)}, u32[]{:S(2)}, u32[]{:S(2)}) async-start(bf16[8,256,512]{2,1,0:T(8,128)(2,1)} %stack.9), calls=%async_computation.1 | async-start | bytes 4194304 | tf_op jit(solution)/shard_map/all_to_all | solution.py:10
  252.8 83.9 %all-reduce.13.cloned.1.call-start = ((), (), s32[]{:S(2)}) async-start(), calls=%async_computation.6 | async-start | bytes 524288 | tf_op jit(solution)/shard_map/psum | solution.py:16
  253.5 212.0 %all-reduce.15.cloned.1.call-start = ((), (), s32[]{:S(2)}) async-start(), calls=%async_computation.7 | async-start | bytes 2097152 | tf_op jit(solution)/shard_map/psum | solution.py:16
  474.5 93.8 %all-to-all-start.2 = ((bf16[8,256,512]{2,1,0:T(8,128)(2,1)}), bf16[8,256,512]{2,1,0:T(8,128)(2,1)}, u32[]{:S(2)}, u32[]{:S(2)}) async-start(bf16[8,256,512]{2,1,0:T(8,128)(2,1)} %stack.10), calls=%async_computation.2 | async-start | bytes 4194304 | tf_op jit(solution)/shard_map/all_to_all | solution.py:10
  481.3 84.0 %all-reduce.17.cloned.1.call-start = ((), (), s32[]{:S(2)}) async-start(), calls=%async_computation.8 | async-start | bytes 524288 | tf_op jit(solution)/shard_map/psum | solution.py:16
  481.9 208.5 %all-reduce.19.cloned.1.call-start = ((), (), s32[]{:S(2)}) async-start(), calls=%async_computation.9 | async-start | bytes 2097152 | tf_op jit(solution)/shard_map/psum | solution.py:16
  704.0 95.8 %all-to-all-start.3 = ((bf16[8,256,512]{2,1,0:T(8,128)(2,1)}), bf16[8,256,512]{2,1,0:T(8,128)(2,1)S(1)}, u32[]{:S(2)}, u32[]{:S(2)}) async-start(bf16[8,256,512]{2,1,0:T(8,128)(2,1)} %stack.11), calls=%async_computation.3 | async-start | bytes 4194304 | tf_op jit(solution)/shard_map/all_to_all | solution.py:10
  710.7 83.9 %all-reduce.21.cloned.1.call-start = ((), (), s32[]{:S(2)}) async-start(), calls=%async_computation.10 | async-start | bytes 524288 | tf_op jit(solution)/shard_map/psum | solution.py:16
  711.5 212.0 %all-reduce.23.cloned.1.call-start = ((), (), s32[]{:S(2)}) async-start(), calls=%async_computation.11 | async-start | bytes 2097152 | tf_op jit(solution)/shard_map/psum | solution.py:16
Sparse Core Ops, SparseCore 0:
  24.6 82.5 all-reduce.8
  113.5 118.9 all-reduce.10
  255.9 80.7 all-reduce.12
  346.7 118.8 all-reduce.14
  484.1 81.1 all-reduce.16
  571.5 118.8 all-reduce.18
  713.9 80.7 all-reduce.20
  804.6 118.8 all-reduce.22
